TPU v7x, 32 devices: a whole 2x2x4 slice. The times are simulated.
32 devices in a mesh: band: 2 (over x), gx: 16 (over z, y, core).
Axes of the slice: x: 2, y: 2, z: 4, core: 2. Of those that a mesh axis runs over, the one named last changes fastest.
Arguments:
- slc_tiles: bfloat16 [64, 2, 64, 2048], P('gx', None, 'band'), parts along dimension 2, may hold values from -64 to 64
- look_weight: float32 [64, 2048], P('band'), parts along dimension 0, may hold values from 0.05 to 1
- pair_list: int32 [192, 2], replicated, may hold values from 0 to 63, as said below
Outputs:
- corrected: float32 [64, 64, 2048], P(None, 'band', 'gx'), parts along dimension 1
There are 2 independent parts, one for each index of `band`. A program takes and returns all parts, laid end to end along the dimension named above; an argument that names none is the same for every part. Nothing has to cross between parts.
Inputs may be any that keep to these rules, and one draw needn't show every extreme that they name: `pair_list`: row p is a pair of date indices; with d = p // 12, the reference date lies in d * 4 to (d + 1) * 4 - 1 and the secondary date is 1 to 4 dates after it.
All inputs are finite; a program needn't handle non-finite values.
Results may differ from a plain program's by a relative error of at most 0.0071.
Values may be sent and summed in bfloat16 or wider, within the bound.
No kernel may reach another device: no remote copies, remote signals or barrier semaphores. Data moves between devices by JAX's collectives and lax.ppermute only.
A program may use at most 128 MiB of HBM per device.

v0:
```python
import jax
import jax.numpy as jnp
from jax import lax
from jax.sharding import PartitionSpec as P

LOOK = 9


def from_behind(block, axis, distance):
    devices = range(lax.axis_size(axis))
    route = [(i - distance, i) for i in devices if i - distance in devices]
    return lax.ppermute(block, axis, route)


def box_sum(values, col_count):
    rim_width = LOOK // 2
    row_count = values.shape[-2]
    padded = jnp.pad(values, [(0, 0)] * (values.ndim - 2) + [(rim_width, rim_width), (0, 0)])
    running = padded[..., 0:row_count, :]
    for offset in range(1, LOOK):
        running = running + padded[..., offset : offset + row_count, :]
    summed = running[..., 0:col_count]
    for offset in range(1, LOOK):
        summed = summed + running[..., offset : offset + col_count]
    return summed


def observe(first_tile, second_tile, weight, col_count):
    first_re = first_tile[..., 0, :, :].astype(jnp.float32)
    first_im = first_tile[..., 1, :, :].astype(jnp.float32)
    second_re = second_tile[..., 0, :, :].astype(jnp.float32)
    second_im = second_tile[..., 1, :, :].astype(jnp.float32)
    cross_re = weight * (first_re * second_re + first_im * second_im)
    cross_im = weight * (first_im * second_re - first_re * second_im)
    power_first = weight * (first_re * first_re + first_im * first_im)
    power_second = weight * (second_re * second_re + second_im * second_im)
    stacked = jnp.stack([cross_re, cross_im, power_first, power_second], axis=0)
    looked = box_sum(stacked, col_count)
    return (looked[1] * lax.rsqrt(looked[2] * looked[3] + 1e-06)).astype(jnp.bfloat16)


def solve_normal(normal_matrix, projected):
    factor = jnp.linalg.cholesky(normal_matrix)
    return jax.scipy.linalg.cho_solve((factor, True), projected)


def body(slc_tiles, look_weight, pair_list):
    rim_width = LOOK // 2
    devices = lax.axis_size("gx")
    position = lax.axis_index("gx")
    date_dev = slc_tiles.shape[0]
    row_count = slc_tiles.shape[2]
    col_total = slc_tiles.shape[3]
    strip_cols = col_total // devices
    pair_total = pair_list.shape[0]
    pair_dev = pair_total // devices
    date_total = date_dev * devices
    weight_pad = jnp.pad(look_weight, ((0, 0), (rim_width, rim_width)))
    following = from_behind(slc_tiles, "gx", -1)
    local_tiles = jnp.concatenate([slc_tiles, following], axis=0)
    local_tiles = jnp.pad(local_tiles, ((0, 0), (0, 0), (0, 0), (rim_width, rim_width)))
    own_pairs = (
        lax.dynamic_slice_in_dim(pair_list, position * pair_dev, pair_dev, 0) - position * date_dev
    )

    def one_pair(pair_row):
        return observe(local_tiles[pair_row[0]], local_tiles[pair_row[1]], weight_pad, col_total)

    observed = lax.map(one_pair, own_pairs)
    blocks = observed.reshape(pair_dev, row_count, devices, strip_cols)
    strips = lax.all_to_all(blocks, "gx", split_axis=2, concat_axis=0, tiled=True)
    strips = strips.reshape(pair_total, row_count * strip_cols)
    date_ids = lax.iota(jnp.int32, date_total)
    incidence = (
        (date_ids[:, None] == pair_list[None, :, 0]).astype(jnp.float32)
        - (date_ids[:, None] == pair_list[None, :, 1]).astype(jnp.float32)
    ).astype(jnp.bfloat16)
    normal_matrix = jnp.dot(incidence, incidence.T, preferred_element_type=jnp.float32) + jnp.eye(
        date_total, dtype=jnp.float32
    )
    projected = jnp.dot(incidence, strips, preferred_element_type=jnp.float32)
    series = solve_normal(normal_matrix, projected).reshape(date_total, row_count, strip_cols)
    column_ids = position * strip_cols + lax.iota(jnp.int32, strip_cols)
    columns = (2.0 * column_ids.astype(jnp.float32) + 1.0) / col_total - 1.0
    all_cols = (2.0 * lax.iota(jnp.int32, col_total).astype(jnp.float32) + 1.0) / col_total - 1.0
    square_sum = jnp.sum(all_cols * all_cols)
    partial_mean = jnp.sum(series, axis=(1, 2))
    partial_slope = jnp.sum(series * columns, axis=(1, 2))
    totals = lax.psum((partial_mean, partial_slope), "gx")
    date_mean = totals[0] / (row_count * col_total)
    date_slope = totals[1] / (row_count * square_sum)
    return series - date_mean[:, None, None] - date_slope[:, None, None] * columns


def solution(mesh):
    return jax.shard_map(
        body,
        mesh=mesh,
        in_specs=(P("gx", None, "band", None), P("band", None), P()),
        out_specs=P(None, "band", "gx"),
        check_vma=False,
    )
```

profile of v0, /device:TPU:0, one launch (start us, length us, event | category | flops | bytes accessed | tf_op | source)
XLA Modules:
  0.0 213.2 jit_solution(9840836476358481530)
XLA Ops:
  0.0 1.3 collective-permute-start
  1.3 1.1 pad.15
  2.4 1.3 dynamic-slice_subtract_fusion
  3.7 1.0 collective-permute-done
  4.8 2.6 %fusion.28 = bf16[8,2,32,2056]{3,2,1,0:T(8,128)(2,1)S(1)} fusion(bf16[4,2,32,2048]{3,2,1,0:T(8,128)(2,1)S(1)} %collective-permute-done, bf16[4,2,32,2048]{3,2,1,0:T(8,128)(2,1)} %param.5), kind=kLoop, calls=%fused_computation.57 | loop fusion | flops 9474048 | bytes 4202496 | tf_op jit(solution)/shard_map/concatenate | solution.py:60
  7.3 108.7 %while.12 = (s32[]{:T(128)}, bf16[12,32,2048]{2,1,0:T(8,128)(2,1)}, f32[32,2056]{1,0:T(8,128)S(1)}, s32[12,2]{0,1:T(2,128)}, bf16[8,2,32,2056]{3,2,1,0:T(8,128)(...) while((s32[]{:T(128)}, bf16[12,32,2048]{2,1,0:T(8,128)(2,1)}, f32[32,2056]{1,0:T(8,128)S(1)}, ...), condition=%wide.region_3.4_spmd, body=%wide.region_2.3_spmd.sunk | while | flops 6569993 | bytes 17456360 | solution.py:69
  7.3 0.8 constant_dynamic-slice_fusion.2
  12.6 0.8 fusion.58
  13.5 2.2 %slice_add_fusion.9 = f32[4,32,2048]{2,1,0:T(8,128)S(1)} fusion(f32[4,32,2056]{2,1,0:T(8,128)S(1)} %fusion.58), kind=kLoop, calls=%fused_computation.17.clone.1 | loop fusion | flops 2097152 | bytes 10485760 | tf_op jit(solution)/shard_map/while/body/eval_jaxpr/add | solution.py:24
  16.4 0.7 constant_dynamic-slice_fusion.2
  21.7 0.8 fusion.58
  22.5 2.2 %slice_add_fusion.9 = f32[4,32,2048]{2,1,0:T(8,128)S(1)} fusion(f32[4,32,2056]{2,1,0:T(8,128)S(1)} %fusion.58), kind=kLoop, calls=%fused_computation.17.clone.1 | loop fusion | flops 2097152 | bytes 10485760 | tf_op jit(solution)/shard_map/while/body/eval_jaxpr/add | solution.py:24
  25.4 0.7 constant_dynamic-slice_fusion.2
  30.7 0.8 fusion.58
  31.6 2.2 %slice_add_fusion.9 = f32[4,32,2048]{2,1,0:T(8,128)S(1)} fusion(f32[4,32,2056]{2,1,0:T(8,128)S(1)} %fusion.58), kind=kLoop, calls=%fused_computation.17.clone.1 | loop fusion | flops 2097152 | bytes 10485760 | tf_op jit(solution)/shard_map/while/body/eval_jaxpr/add | solution.py:24
  34.5 0.7 constant_dynamic-slice_fusion.2
  39.8 0.8 fusion.58
  40.6 2.2 %slice_add_fusion.9 = f32[4,32,2048]{2,1,0:T(8,128)S(1)} fusion(f32[4,32,2056]{2,1,0:T(8,128)S(1)} %fusion.58), kind=kLoop, calls=%fused_computation.17.clone.1 | loop fusion | flops 2097152 | bytes 10485760 | tf_op jit(solution)/shard_map/while/body/eval_jaxpr/add | solution.py:24
  43.6 0.7 constant_dynamic-slice_fusion.2
  48.9 0.8 fusion.58
  49.7 2.2 %slice_add_fusion.9 = f32[4,32,2048]{2,1,0:T(8,128)S(1)} fusion(f32[4,32,2056]{2,1,0:T(8,128)S(1)} %fusion.58), kind=kLoop, calls=%fused_computation.17.clone.1 | loop fusion | flops 2097152 | bytes 10485760 | tf_op jit(solution)/shard_map/while/body/eval_jaxpr/add | solution.py:24
  57.9 0.8 fusion.58
  58.7 2.2 %slice_add_fusion.9 = f32[4,32,2048]{2,1,0:T(8,128)S(1)} fusion(f32[4,32,2056]{2,1,0:T(8,128)S(1)} %fusion.58), kind=kLoop, calls=%fused_computation.17.clone.1 | loop fusion | flops 2097152 | bytes 10485760 | tf_op jit(solution)/shard_map/while/body/eval_jaxpr/add | solution.py:24
  61.7 0.7 constant_dynamic-slice_fusion.2
  67.0 0.8 fusion.58
  67.8 2.2 %slice_add_fusion.9 = f32[4,32,2048]{2,1,0:T(8,128)S(1)} fusion(f32[4,32,2056]{2,1,0:T(8,128)S(1)} %fusion.58), kind=kLoop, calls=%fused_computation.17.clone.1 | loop fusion | flops 2097152 | bytes 10485760 | tf_op jit(solution)/shard_map/while/body/eval_jaxpr/add | solution.py:24
  70.7 0.7 constant_dynamic-slice_fusion.2
  76.0 0.8 fusion.58
  76.8 2.2 %slice_add_fusion.9 = f32[4,32,2048]{2,1,0:T(8,128)S(1)} fusion(f32[4,32,2056]{2,1,0:T(8,128)S(1)} %fusion.58), kind=kLoop, calls=%fused_computation.17.clone.1 | loop fusion | flops 2097152 | bytes 10485760 | tf_op jit(solution)/shard_map/while/body/eval_jaxpr/add | solution.py:24
  79.8 0.7 constant_dynamic-slice_fusion.2
  85.1 0.8 fusion.58
  85.9 2.2 %slice_add_fusion.9 = f32[4,32,2048]{2,1,0:T(8,128)S(1)} fusion(f32[4,32,2056]{2,1,0:T(8,128)S(1)} %fusion.58), kind=kLoop, calls=%fused_computation.17.clone.1 | loop fusion | flops 2097152 | bytes 10485760 | tf_op jit(solution)/shard_map/while/body/eval_jaxpr/add | solution.py:24
  94.1 0.8 fusion.58
  95.0 2.2 %slice_add_fusion.9 = f32[4,32,2048]{2,1,0:T(8,128)S(1)} fusion(f32[4,32,2056]{2,1,0:T(8,128)S(1)} %fusion.58), kind=kLoop, calls=%fused_computation.17.clone.1 | loop fusion | flops 2097152 | bytes 10485760 | tf_op jit(solution)/shard_map/while/body/eval_jaxpr/add | solution.py:24
  103.2 0.8 fusion.58
  104.0 2.2 %slice_add_fusion.9 = f32[4,32,2048]{2,1,0:T(8,128)S(1)} fusion(f32[4,32,2056]{2,1,0:T(8,128)S(1)} %fusion.58), kind=kLoop, calls=%fused_computation.17.clone.1 | loop fusion | flops 2097152 | bytes 10485760 | tf_op jit(solution)/shard_map/while/body/eval_jaxpr/add | solution.py:24
  112.3 0.8 fusion.58
  113.1 2.2 %slice_add_fusion.9 = f32[4,32,2048]{2,1,0:T(8,128)S(1)} fusion(f32[4,32,2056]{2,1,0:T(8,128)S(1)} %fusion.58), kind=kLoop, calls=%fused_computation.17.clone.1 | loop fusion | flops 2097152 | bytes 10485760 | tf_op jit(solution)/shard_map/while/body/eval_jaxpr/add | solution.py:24
  116.0 3.0 %copy_bitcast_fusion = bf16[12,32,16,128]{3,1,0,2:T(8,128)(2,1)} fusion(bf16[12,32,2048]{2,1,0:T(8,128)(2,1)} %get-tuple-element.70), kind=kLoop, calls=%fused_computation.62 | loop fusion | bytes 3145728 | tf_op jit(solution)/shard_map/reshape | solution.py:70
  119.0 18.4 %all-to-all-start = ((bf16[12,32,16,128]{3,1,0,2:T(8,128)(2,1)}), bf16[12,32,16,128]{3,1,0,2:T(8,128)(2,1)S(1)}, u32[]{:S(2)}, u32[]{:S(2)}) async-start(bf16[12,32,16,128]{3,1,0,2:T(8,128)(2,1)} %copy_bitcast_fusion), calls=%async_computation | async-start | bytes 3145728 | tf_op jit(solution)/shard_map/all_to_all | solution.py:71
  137.7 5.8 %cholesky.17 = f32[64,64]{1,0:T(8,128)S(1)} custom-call(f32[64,64]{1,0:T(8,128)S(1)} %fusion.41), custom_call_target="Cholesky" | custom-call | tf_op jit(solution)/shard_map/jit(cholesky)/cholesky | solution.py:43
  144.9 4.9 %custom-call.10 = f32[1,64,64]{1,2,0:T(8,128)S(1)} custom-call(f32[1,64,64]{2,1,0:T(8,128)S(1)} %fusion.34), custom_call_target="InvertDiagBlocksLowerTriangular" | custom-call | tf_op jit(solution)/shard_map/jit(_cho_solve)/triangular_solve | solution.py:44
  151.1 18.2 %all-to-all-done = bf16[12,32,16,128]{3,1,0,2:T(8,128)(2,1)S(1)} async-done(((bf16[12,32,16,128]{3,1,0,2:T(8,128)(2,1)}), bf16[12,32,16,128]{3,1,0,2:T(8,128)(2,1)S(1)}, u32[]{:S(2)}, u32[]{:S(2)}) %all-to-all-start) | async-done | bytes 1572896 | tf_op jit(solution)/shard_map/all_to_all | solution.py:71
  169.3 1.2 fusion.29
  170.5 2.5 %fusion.38 = f32[32,128,64]{1,2,0:T(8,128)S(1)} fusion(f32[32,128,64]{2,1,0:T(8,128)S(1)} %fusion.29, f32[1,64,64]{1,2,0:T(8,128)S(1)} %custom-call.10), kind=kOutput, calls=%fused_computation.74 | convolution fusion | flops 201326592 | bytes 2113536 | tf_op jit(solution)/shard_map/jit(_cho_solve)/triangular_solve | solution.py:44
  173.0 1.2 fusion.46
  174.2 37.2 %all-reduce.3 = (f32[64]{0:T(128)S(1)}, f32[64]{0:T(128)S(1)}) all-reduce(f32[64]{0:T(128)S(1)} %get-tuple-element.72, f32[64]{0:T(128)S(1)} %get-tuple-element.71), channel_id=1, replica_groups=mesh['band'=2,'gx'=16] {'gx'}, use_global_device_ids=true, to_apply=%region_7.8 | all-reduce | flops 128 | bytes 1024 | tf_op jit(solution)/shard_map/psum | solution.py:89
  211.7 1.6 copy.8
  (67 shorter events, 23.7 us)
Async XLA Ops:
  0.0 4.8 %collective-permute-start = (bf16[4,2,32,2048]{3,2,1,0:T(8,128)(2,1)}, bf16[4,2,32,2048]{3,2,1,0:T(8,128)(2,1)S(1)}, u32[]{:S(2)}, u32[]{:S(2)}) collective-permute-start(bf16[4,2,32,2048]{3,2,1,0:T(8,128)(2,1)} %param.5), channel_id=1, source_target_pairs={{1,0},{2,1},{3,2},{4,3},{5,4},{6,5},{7,6},{8,7},{9,8},{10,9},{11,1... | collective-permute-start | bytes 3145736 | tf_op jit(solution)/shard_map/ppermute | solution.py:12
  119.0 18.4 %copy-start = (s32[192,2]{0,1:T(2,128)S(1)}, s32[192,2]{0,1:T(2,128)}, u32[]{:S(2)}) copy-start(s32[192,2]{0,1:T(2,128)} %param.7) | copy-start | bytes 4612
  119.0 50.3 %all-to-all-start = ((bf16[12,32,16,128]{3,1,0,2:T(8,128)(2,1)}), bf16[12,32,16,128]{3,1,0,2:T(8,128)(2,1)S(1)}, u32[]{:S(2)}, u32[]{:S(2)}) async-start(bf16[12,32,16,128]{3,1,0,2:T(8,128)(2,1)} %copy_bitcast_fusion), calls=%async_computation | async-start | bytes 3145728 | tf_op jit(solution)/shard_map/all_to_all | solution.py:71
where the time goes:
time: 214 us; the launch traced here: 213 us
  other arithmetic  65.1 us (30%)
  loops' own time  45 us (21%)
  blocking collectives  37.2 us (17%)
  local copies, waits for them, and re-layouts  21.2 us (10%)
  starting transfers between devices  19.7 us (9%)
  waiting for transfers between devices  19.2 us (9%)
  matrix products  5.02 us (2%)
    another operation x1, loops' own time, body(): observed = lax.map(one_pair, own_pairs)  45 us
    psum x1, blocking collectives, body(): totals = lax.psum((partial_mean, partial_slope), 'gx')  37.2 us
    add x12, other arithmetic, box_sum(): summed = summed + running[..., offset:offset + col_count]  26.7 us
    all_to_all x1, starting transfers between devices, body(): lax.all_to_all(blocks, 'gx', split_axis=2, concat_axis=0, tiled=True)  18.4 us
    all_to_all x1, waiting for transfers between devices, body(): lax.all_to_all(blocks, 'gx', split_axis=2, concat_axis=0, tiled=True)  18.2 us
    add x12, other arithmetic, box_sum(): running = running + padded[..., offset:offset + row_count, :]  9.79 us
    dynamic_slice x12, local copies, waits for them, and re-layouts, body(): observed = lax.map(one_pair, own_pairs)  9 us
    dynamic_update_slice x12, other arithmetic, body(): observed = lax.map(one_pair, own_pairs)  8.45 us
  transfers between devices with their start and end apart: 2, of which 2 were waited for; matrix products, arithmetic and copies ran while one was open for 7% of the time, Pallas kernels for 0%

commit v1 on v0

--- a/solution.py
+++ b/solution.py
@@ -2,6 +2,7 @@
 import jax.numpy as jnp
 from jax import lax
 from jax.sharding import PartitionSpec as P
+from jax.lax import all_to_all, psum
 
 LOOK = 9
 
@@ -68,7 +69,11 @@
 
     observed = lax.map(one_pair, own_pairs)
     blocks = observed.reshape(pair_dev, row_count, devices, strip_cols)
-    strips = lax.all_to_all(blocks, "gx", split_axis=2, concat_axis=0, tiled=True)
+    arr_next = psum(1, "gx")
+    w1 = jnp.split(blocks, arr_next, 2)
+    long_array = jnp.stack(w1, axis=0)
+    base_arr = all_to_all(long_array, "gx", 0, 0)
+    strips = jnp.concatenate(base_arr, 0)
     strips = strips.reshape(pair_total, row_count * strip_cols)
     date_ids = lax.iota(jnp.int32, date_total)
     incidence = (

time: 214 us -> 225 us (1.051)
  local copies, waits for them, and re-layouts: 21.2 us -> 34 us
    unnamed x2 -> x18, local copies, waits for them, and re-layouts: 0.01 us -> 11.5 us
    split x0 -> x1, local copies, waits for them, and re-layouts: none -> 3.6 us  [body(): w1 = jnp.split(blocks, arr_next, 2)]
    reshape x1 -> x0, local copies, waits for them, and re-layouts: 2.96 us -> none  [body(): blocks = observed.reshape(pair_dev, row_count, devices, strip_cols)]
where the time goes in v1:
time: 225 us; the launch traced here: 224 us
  other arithmetic  65.1 us (29%)
  loops' own time  45 us (20%)
  blocking collectives  37.2 us (17%)
  local copies, waits for them, and re-layouts  34 us (15%)
  starting transfers between devices  19.7 us (9%)
  waiting for transfers between devices  19.2 us (9%)
  matrix products  2.98 us (1%)
    another operation x1, loops' own time, body(): observed = lax.map(one_pair, own_pairs)  45 us
    psum x1, blocking collectives, body(): totals = lax.psum((partial_mean, partial_slope), 'gx')  37.2 us
    add x12, other arithmetic, box_sum(): summed = summed + running[..., offset:offset + col_count]  26.7 us
    all_to_all x1, starting transfers between devices, body(): base_arr = all_to_all(long_array, 'gx', 0, 0)  18.4 us
    all_to_all x1, waiting for transfers between devices, body(): base_arr = all_to_all(long_array, 'gx', 0, 0)  18.2 us
    unnamed x18, local copies, waits for them, and re-layouts  11.5 us
    add x12, other arithmetic, box_sum(): running = running + padded[..., offset:offset + row_count, :]  9.79 us
    dynamic_slice x12, local copies, waits for them, and re-layouts, body(): observed = lax.map(one_pair, own_pairs)  9 us
  transfers between devices with their start and end apart: 2, of which 2 were waited for; matrix products, arithmetic and copies ran while one was open for 7% of the time, Pallas kernels for 0%

profile of v1, /device:TPU:0, one launch (start us, length us, event | category | flops | bytes accessed | tf_op | source)
XLA Modules:
  0.0 224.0 jit_solution(3601049841131053343)
XLA Ops:
  0.0 1.3 collective-permute-start
  1.3 1.1 pad.15
  2.4 1.3 dynamic-slice_subtract_fusion
  3.7 1.0 collective-permute-done
  4.8 2.6 %fusion.28 = bf16[8,2,32,2056]{3,2,1,0:T(8,128)(2,1)S(1)} fusion(bf16[4,2,32,2048]{3,2,1,0:T(8,128)(2,1)S(1)} %collective-permute-done, bf16[4,2,32,2048]{3,2,1,0:T(8,128)(2,1)} %param.5), kind=kLoop, calls=%fused_computation.57 | loop fusion | flops 9474048 | bytes 4202496 | tf_op jit(solution)/shard_map/concatenate | solution.py:61
  7.3 108.7 %while.12 = (s32[]{:T(128)}, bf16[12,32,2048]{2,1,0:T(8,128)(2,1)}, f32[32,2056]{1,0:T(8,128)S(1)}, s32[12,2]{0,1:T(2,128)}, bf16[8,2,32,2056]{3,2,1,0:T(8,128)(...) while((s32[]{:T(128)}, bf16[12,32,2048]{2,1,0:T(8,128)(2,1)}, f32[32,2056]{1,0:T(8,128)S(1)}, ...), condition=%wide.region_3.4_spmd, body=%wide.region_2.3_spmd.sunk | while | flops 6569993 | bytes 17456860 | solution.py:70
  7.3 0.8 constant_dynamic-slice_fusion.2
  12.6 0.8 fusion.58
  13.5 2.2 slice_add_fusion.9
  21.7 0.8 fusion.58
  22.5 2.2 slice_add_fusion.9
  25.4 0.7 constant_dynamic-slice_fusion.2
  30.7 0.8 fusion.58
  31.6 2.2 slice_add_fusion.9
  34.5 0.7 constant_dynamic-slice_fusion.2
  39.8 0.8 fusion.58
  40.6 2.2 slice_add_fusion.9
  48.9 0.8 fusion.58
  49.7 2.2 slice_add_fusion.9
  52.6 0.7 constant_dynamic-slice_fusion.2
  57.9 0.8 fusion.58
  58.7 2.2 slice_add_fusion.9
  61.7 0.7 constant_dynamic-slice_fusion.2
  67.0 0.8 fusion.58
  67.8 2.2 slice_add_fusion.9
  76.0 0.8 fusion.58
  76.8 2.2 slice_add_fusion.9
  85.1 0.8 fusion.58
  85.9 2.2 slice_add_fusion.9
  88.8 0.7 constant_dynamic-slice_fusion.2
  94.1 0.8 fusion.58
  95.0 2.2 slice_add_fusion.9
  97.9 0.7 constant_dynamic-slice_fusion.2
  103.2 0.8 fusion.58
  104.0 2.2 slice_add_fusion.9
  106.9 0.7 constant_dynamic-slice_fusion.2
  112.3 0.8 fusion.58
  113.1 2.2 slice_add_fusion.9
  116.0 1.8 copy.210
  117.8 3.6 %fusion.48 = (bf16[12,32,1,128]{3,2,1,0:T(2,128)(2,1)S(1)}, bf16[12,32,1,128]{3,2,1,0:T(2,128)(2,1)S(1)}, bf16[12,32,1,128]{3,2,1,0:T(2,128)(2,1)S(1)}, bf16[12,...) fusion(bf16[12,32,16,128]{3,2,1,0:T(8,128)(2,1)S(1)} %bitcast.107), kind=kLoop, calls=%fused_computation.111 | loop fusion | bytes 3145728 | tf_op jit(solution)/shard_map/split | solution.py:73
  131.8 18.4 %all-to-all-start = ((bf16[16,12,32,1,128]{4,2,1,3,0:T(8,128)(2,1)}), bf16[16,12,32,1,128]{4,2,1,3,0:T(8,128)(2,1)S(1)}, u32[]{:S(2)}, u32[]{:S(2)}) async-start(bf16[16,12,32,1,128]{4,2,1,3,0:T(8,128)(2,1)} %bitcast_dynamic-update-slice_fusion), calls=%async_computation | async-start | bytes 3145728 | tf_op jit(solution)/shard_map/all_to_all | solution.py:75
  150.5 5.8 %cholesky.17 = f32[64,64]{1,0:T(8,128)S(1)} custom-call(f32[64,64]{1,0:T(8,128)S(1)} %fusion.41), custom_call_target="Cholesky" | custom-call | tf_op jit(solution)/shard_map/jit(cholesky)/cholesky | solution.py:44
  157.7 4.9 %custom-call.10 = f32[1,64,64]{1,2,0:T(8,128)S(1)} custom-call(f32[1,64,64]{2,1,0:T(8,128)S(1)} %fusion.34), custom_call_target="InvertDiagBlocksLowerTriangular" | custom-call | tf_op jit(solution)/shard_map/jit(_cho_solve)/triangular_solve | solution.py:45
  163.9 18.2 %all-to-all-done = bf16[16,12,32,1,128]{4,2,1,3,0:T(8,128)(2,1)S(1)} async-done(((bf16[16,12,32,1,128]{4,2,1,3,0:T(8,128)(2,1)}), bf16[16,12,32,1,128]{4,2,1,3,0:T(8,128)(2,1)S(1)}, u32[]{:S(2)}, u32[]{:S(2)}) %all-to-all-start) | async-done | bytes 1572896 | tf_op jit(solution)/shard_map/all_to_all | solution.py:75
  182.7 1.1 fusion.36
  183.8 1.1 fusion.46
  184.9 37.2 %all-reduce.3 = (f32[64]{0:T(128)S(1)}, f32[64]{0:T(128)S(1)}) all-reduce(f32[64]{0:T(128)S(1)} %get-tuple-element.72, f32[64]{0:T(128)S(1)} %get-tuple-element.71), channel_id=1, replica_groups=mesh['band'=2,'gx'=16] {'gx'}, use_global_device_ids=true, to_apply=%region_7.8 | all-reduce | flops 128 | bytes 1024 | tf_op jit(solution)/shard_map/psum | solution.py:94
  222.5 1.6 copy.190
  (84 shorter events, 34.8 us)
Async XLA Ops:
  0.0 4.8 %collective-permute-start = (bf16[4,2,32,2048]{3,2,1,0:T(8,128)(2,1)}, bf16[4,2,32,2048]{3,2,1,0:T(8,128)(2,1)S(1)}, u32[]{:S(2)}, u32[]{:S(2)}) collective-permute-start(bf16[4,2,32,2048]{3,2,1,0:T(8,128)(2,1)} %param.5), channel_id=1, source_target_pairs={{1,0},{2,1},{3,2},{4,3},{5,4},{6,5},{7,6},{8,7},{9,8},{10,9},{11,1... | collective-permute-start | bytes 3145736 | tf_op jit(solution)/shard_map/ppermute | solution.py:13
  131.8 18.4 %copy-start = (s32[192,2]{0,1:T(2,128)S(1)}, s32[192,2]{0,1:T(2,128)}, u32[]{:S(2)}) copy-start(s32[192,2]{0,1:T(2,128)} %param.7) | copy-start | bytes 4612
  131.8 50.3 %all-to-all-start = ((bf16[16,12,32,1,128]{4,2,1,3,0:T(8,128)(2,1)}), bf16[16,12,32,1,128]{4,2,1,3,0:T(8,128)(2,1)S(1)}, u32[]{:S(2)}, u32[]{:S(2)}) async-start(bf16[16,12,32,1,128]{4,2,1,3,0:T(8,128)(2,1)} %bitcast_dynamic-update-slice_fusion), calls=%async_computation | async-start | bytes 3145728 | tf_op jit(solution)/shard_map/all_to_all | solution.py:75
